TPU v7x, 32 devices: a whole 2x2x4 slice. The times are simulated.
32 devices in a mesh: cluster: 2 (over x), sub: 16 (over z, y, core).
Axes of the slice: x: 2, y: 2, z: 4, core: 2. Of those that a mesh axis runs over, the one named last changes fastest.
Arguments:
- load_terms: float32 [32, 128, 1536], P(('cluster', 'sub')), may hold values from -60 to 60
- dual_operator: bfloat16 [32, 1536, 1536], P(('cluster', 'sub')), may hold values from -2 to 16, as said below
- dirichlet: bfloat16 [32, 1536, 1536], P(('cluster', 'sub')), may hold values from -2 to 16, as said below
- corner_coupling: bfloat16 [32, 1536, 24], P(('cluster', 'sub')), may hold values from -0.25 to 0.25
- coarse_inverse: float32 [96, 96], P(('cluster', 'sub')), may hold values from -2 to 4, as said below
- face_map: int32 [32, 6, 256], P(('cluster', 'sub')), may hold values from 0 to 255, as said below
- face_live: int32 [32, 6], P(('cluster', 'sub')), may hold values from 0 to 1, as said below
- corner_ids: int32 [32, 8], P(('cluster', 'sub')), may hold values from 0 to 31, as said below
Outputs:
- multipliers: float32 [32, 128, 1536], P(('cluster', 'sub'))
- residual: float32 [32, 128, 1536], P(('cluster', 'sub'))
Inputs may be any that keep to these rules, and one draw needn't show every extreme that they name: face_map[d, f] is a permutation of the slots of a face; the maps of the two sides of a face pair are inverse to each other. `face_live`: equal on the two sides of a face pair. `corner_ids`: the eight corners of a subdomain are the lattice vertices (c + a, s + b + 4 * e) for a, b, e in 0 and 1, taken modulo 2 and 16; each vertex has one number and is shared by eight subdomains. `dual_operator`: each subdomain's matrix is symmetric and positive definite. `dirichlet`: each subdomain's matrix is symmetric and positive definite. `coarse_inverse`: symmetric and positive definite.
All inputs are finite; a program needn't handle non-finite values.
Results may differ from a plain program's by a relative error of at most 0.0099.
Values sent between devices are 32-bit elements; how exact they have to be, the bound alone decides.
No kernel may reach another device: no remote copies, remote signals or barrier semaphores. Data moves between devices by JAX's collectives and lax.ppermute only.
A program may use at most 128 MiB of HBM per device.

v0:
```python
import jax
import jax.numpy as jnp
from jax import lax
from jax.sharding import PartitionSpec as P

ITERS = 2
STRIDE = 4


def padded(block, sides, width):
    for axis, dim in sides:
        count = lax.axis_size(axis)
        forward = [(i, i + 1) for i in range(count - 1)]
        forward.append((count - 1, 0))
        backward = [(target, source) for source, target in forward]
        low = lax.ppermute(
            lax.slice_in_dim(block, block.shape[dim] - width, None, axis=dim), axis, forward
        )
        high = lax.ppermute(lax.slice_in_dim(block, 0, width, axis=dim), axis, backward)
        block = jnp.concatenate([low, block, high], axis=dim)
    return block


def passed_along(value, axis, steps):
    count = lax.axis_size(axis)
    pairs = [(source, (source + steps) % count) for source in range(count)]
    return lax.ppermute(value, axis, pairs)


def local(
    load_terms,
    dual_operator,
    dirichlet,
    corner_coupling,
    coarse_inverse,
    face_map,
    face_live,
    corner_ids,
):
    local_loads = load_terms[0]
    operator_local = dual_operator[0]
    precond_local = dirichlet[0]
    coupling = corner_coupling[0]
    slot_maps = face_map[0]
    live_faces = face_live[0].astype(jnp.float32)
    corners = corner_ids[0]
    load_count = local_loads.shape[0]
    dual_size = local_loads.shape[1]
    face_size = dual_size // 6
    coarse_size = coarse_inverse.shape[1]
    coarse_index = (3 * corners[:, None] + jnp.arange(3, dtype=jnp.int32)[None, :]).reshape(-1)
    spread = (coarse_index[:, None] == jnp.arange(coarse_size, dtype=jnp.int32)[None, :]).astype(
        jnp.float32
    )

    def assemble(local_sum):
        face_parts = local_sum.reshape(load_count, 6, face_size)
        slab_pair = padded(jnp.stack([face_parts[:, 0], face_parts[:, 1]]), (("cluster", 0),), 1)
        row_pair = padded(jnp.stack([face_parts[:, 2], face_parts[:, 3]]), (("sub", 0),), 1)
        column_pair = []
        for source_face, shift_step in ((5, STRIDE), (4, -STRIDE)):
            column_pair.append(passed_along(face_parts[:, source_face], "sub", shift_step))
        received = [
            slab_pair[0],
            slab_pair[3],
            row_pair[0],
            row_pair[3],
            column_pair[0],
            column_pair[1],
        ]
        pieces = []
        for face_index in range(6):
            permuted = jnp.take(received[face_index], slot_maps[face_index], axis=1)
            pieces.append((face_parts[:, face_index] + permuted) * live_faces[face_index])
        return jnp.concatenate(pieces, axis=1)

    def precond_with_product(vector):
        local_term = jnp.dot(
            vector.astype(jnp.bfloat16), precond_local, preferred_element_type=jnp.float32
        )
        precond = assemble(local_term)
        product = 0.5 * lax.psum(jnp.sum(vector * precond, axis=1), ("cluster", "sub"))
        return (precond, product)

    right_side = assemble(local_loads)
    multipliers = jnp.zeros_like(right_side)
    residual = right_side
    precond, residual_dot = precond_with_product(residual)
    direction = precond
    for iteration in range(ITERS):
        rounded = direction.astype(jnp.bfloat16)
        direct = jnp.dot(rounded, operator_local, preferred_element_type=jnp.float32)
        corner_terms = jnp.dot(rounded, coupling, preferred_element_type=jnp.float32)
        coarse_local = jnp.dot(corner_terms, spread, precision=lax.Precision.HIGHEST)
        local_curve = jnp.sum(direction * direct, axis=1)
        apply_coarse_load, curve_total = lax.psum((coarse_local, local_curve), ("cluster", "sub"))
        own_values = jnp.dot(apply_coarse_load, coarse_inverse.T, precision=lax.Precision.HIGHEST)
        solution = lax.all_gather(own_values, ("cluster", "sub"), axis=1, tiled=True)
        corner_values = jnp.dot(solution, spread.T, precision=lax.Precision.HIGHEST).astype(
            jnp.bfloat16
        )
        back = lax.dot_general(
            corner_values, coupling, (((1,), (1,)), ((), ())), preferred_element_type=jnp.float32
        )
        dual_image = assemble(direct + back)
        curvature = curve_total + jnp.sum(apply_coarse_load * solution, axis=1)
        dual_image, curvature = (dual_image, curvature)
        step_size = residual_dot / curvature
        multipliers = multipliers + step_size[:, None] * direction
        residual = residual - step_size[:, None] * dual_image
        if iteration + 1 < ITERS:
            precond, residual_new = precond_with_product(residual)
            direction = precond + (residual_new / residual_dot)[:, None] * direction
            residual_dot = residual_new
    return (multipliers[None], residual[None])


def solution(mesh):
    placed = (
        P(("cluster", "sub"), None, None),
        P(("cluster", "sub"), None, None),
        P(("cluster", "sub"), None, None),
        P(("cluster", "sub"), None, None),
        P(("cluster", "sub"), None),
        P(("cluster", "sub"), None, None),
        P(("cluster", "sub"), None),
        P(("cluster", "sub"), None),
    )
    return jax.shard_map(
        local,
        mesh=mesh,
        in_specs=placed,
        out_specs=(P(("cluster", "sub"), None, None), P(("cluster", "sub"), None, None)),
        check_vma=False,
    )
```

profile of v0, /device:TPU:0, one launch (start us, length us, event | category | flops | bytes accessed | tf_op | source)
XLA Modules:
  0.0 432.1 jit_solution(1258101771140866283)
XLA Ops:
  2.3 3.0 collective-permute-start
  5.8 4.5 %collective-permute-start.3 = (f32[1,128,256]{2,1,0:T(8,128)S(1)}, f32[1,128,256]{2,1,0:T(8,128)S(1)}, u32[]{:S(2)}, u32[]{:S(2)}) collective-permute-start(f32[1,128,256]{2,1,0:T(8,128)S(1)} %bitcast.561), channel_id=1, source_target_pairs={{1,0},{2,1},{3,2},{4,3},{5,4},{6,5},{7,6},{8,7},{9,8},{10,9},{11,1... | collective-permute-start | bytes 393224 | tf_op jit(solution)/shard_map/ppermute | solution.py:19
  12.5 3.6 collective-permute-start.5
  16.1 6.6 %copy.173 = bf16[1,1536,1536]{1,2,0:T(8,128)(2,1)} copy(bf16[1,1536,1536]{2,1,0:T(8,128)(2,1)} %param.12) | data formatting | bytes 9437184 | tf_op args[2]
  33.2 4.0 fusion.6
  37.3 2.1 collective-permute-start.6
  39.4 4.4 %collective-permute-start.9 = (f32[1,128,256]{2,1,0:T(8,128)S(1)}, f32[1,128,256]{2,1,0:T(8,128)S(1)}, u32[]{:S(2)}, u32[]{:S(2)}) collective-permute-start(f32[1,128,256]{2,1,0:T(8,128)S(1)} %get-tuple-element.30), channel_id=1, source_target_pairs={{1,0},{2,1},{3,2},{4,3},{5,4},{6,5},{7,6},{8,7},{9,8},{10,9},{11,1... | collective-permute-start | bytes 393224 | tf_op jit(solution)/shard_map/ppermute | solution.py:19
  44.0 3.9 collective-permute-start.11
  60.1 3.8 multiply_reduce_fusion.3
  65.1 37.5 %all-reduce.1 = (f32[128,96]{0,1:T(8,128)S(1)}, f32[128]{0:T(128)}, f32[128]{0:T(128)}) all-reduce(f32[128,96]{0,1:T(8,128)} %fusion.53, f32[128]{0:T(128)} %get-tuple-element.4, f32[128]{0:T(128)} %get-tuple-element.3), channel_id=1, replica_groups=mesh['cluster'=2,'sub'=16] {'cluster','sub'}, use_global_device_ids=true, to_apply=%region_4.6 | all-reduce | flops 12544 | bytes 100352 | tf_op jit(solution)/shard_map/psum | solution.py:96
  103.4 41.8 %all-gather = f32[32,3,128]{2,1,0:T(4,128)S(1)} all-gather(f32[1,3,128]{2,1,0:T(4,128)S(1)} %convolution_bitcast_fusion.1), channel_id=1, replica_groups=mesh['cluster'=2,'sub'=16] {'cluster','sub'}, dimensions={0}, use_global_device_ids=true | all-gather | bytes 50688 | tf_op jit(solution)/shard_map/all_gather | solution.py:98
  152.3 2.0 collective-permute-start.13
  155.5 4.5 %collective-permute-start.15 = (f32[1,128,256]{2,1,0:T(8,128)S(1)}, f32[1,128,256]{2,1,0:T(8,128)}, u32[]{:S(2)}, u32[]{:S(2)}) collective-permute-start(f32[1,128,256]{2,1,0:T(8,128)S(1)} %bitcast.568), channel_id=1, source_target_pairs={{1,0},{2,1},{3,2},{4,3},{5,4},{6,5},{7,6},{8,7},{9,8},{10,9},{11,1... | collective-permute-start | bytes 393224 | tf_op jit(solution)/shard_map/ppermute | solution.py:19
  162.1 4.0 collective-permute-start.17
  172.5 1.7 copy.192
  176.6 1.7 copy.196
  180.6 1.7 copy.198
  185.6 2.3 constant_dynamic-update-slice_fusion.17
  191.3 2.2 constant_dynamic-update-slice_fusion.16
  193.5 2.3 constant_dynamic-update-slice_fusion.15
  195.7 2.1 constant_dynamic-update-slice_fusion.14
  200.6 4.3 fusion.4
  205.8 1.9 collective-permute-start.19
  207.7 4.4 %collective-permute-start.21 = (f32[1,128,256]{2,1,0:T(8,128)}, f32[1,128,256]{2,1,0:T(8,128)}, u32[]{:S(2)}, u32[]{:S(2)}) collective-permute-start(f32[1,128,256]{2,1,0:T(8,128)} %get-tuple-element.18), channel_id=1, source_target_pairs={{1,0},{2,1},{3,2},{4,3},{5,4},{6,5},{7,6},{8,7},{9,8},{10,9},{11,1... | collective-permute-start | bytes 393224 | tf_op jit(solution)/shard_map/ppermute | solution.py:19
  212.2 3.8 collective-permute-start.23
  218.4 1.7 copy.206
  222.4 1.7 copy.208
  226.4 1.7 copy.210
  230.4 1.7 copy.212
  236.1 2.2 constant_dynamic-update-slice_fusion.23
  241.6 2.2 constant_dynamic-update-slice_fusion.22
  243.8 2.2 constant_dynamic-update-slice_fusion.21
  246.1 2.1 constant_dynamic-update-slice_fusion.20
  248.2 2.2 constant_dynamic-update-slice_fusion.19
  251.8 1.7 multiply_reduce_fusion.1
  253.5 36.9 %psum.45 = f32[128]{0:T(128)S(1)} all-reduce(f32[128]{0:T(128)S(1)} %multiply_reduce_fusion.1), channel_id=1, replica_groups=mesh['cluster'=2,'sub'=16] {'cluster','sub'}, use_global_device_ids=true, to_apply=%region_7.9 | all-reduce | flops 128 | bytes 1024 | tf_op jit(solution)/shard_map/psum | solution.py:82
  292.4 4.3 multiply_reduce_fusion
  297.0 41.7 %all-reduce = (f32[128]{0:T(128)}, f32[128,96]{0,1:T(8,128)S(1)}) all-reduce(f32[128]{0:T(128)} %get-tuple-element.85, f32[128,96]{0,1:T(8,128)S(1)} %fusion.52), channel_id=1, replica_groups=mesh['cluster'=2,'sub'=16] {'cluster','sub'}, use_global_device_ids=true, to_apply=%region_9.11 | all-reduce | flops 12416 | bytes 99328 | tf_op jit(solution)/shard_map/psum | solution.py:96
  338.8 41.1 %all-gather.1 = f32[32,3,128]{2,1,0:T(4,128)S(1)} all-gather(f32[1,3,128]{2,1,0:T(4,128)S(1)} %convolution_bitcast_fusion), channel_id=1, replica_groups=mesh['cluster'=2,'sub'=16] {'cluster','sub'}, dimensions={0}, use_global_device_ids=true | all-gather | bytes 50688 | tf_op jit(solution)/shard_map/all_gather | solution.py:98
  384.5 1.9 collective-permute-start.25
  388.5 4.5 %collective-permute-start.27 = (f32[1,128,256]{2,1,0:T(8,128)S(1)}, f32[1,128,256]{2,1,0:T(8,128)}, u32[]{:S(2)}, u32[]{:S(2)}) collective-permute-start(f32[1,128,256]{2,1,0:T(8,128)S(1)} %bitcast.573), channel_id=1, source_target_pairs={{1,0},{2,1},{3,2},{4,3},{5,4},{6,5},{7,6},{8,7},{9,8},{10,9},{11,1... | collective-permute-start | bytes 393224 | tf_op jit(solution)/shard_map/ppermute | solution.py:19
  395.5 3.8 collective-permute-start.29
  414.4 1.7 copy.235
  416.1 2.8 bitcast_dynamic-update-slice_fusion.10
  418.9 2.7 bitcast_dynamic-update-slice_fusion.9
  421.7 2.6 bitcast_dynamic-update-slice_fusion.8
  424.3 2.4 bitcast_dynamic-update-slice_fusion.7
  428.3 3.8 multiply_subtract_fusion
  (373 shorter events, 106.2 us)
Async XLA Ops:
  0.6 63.3 %copy-start = (bf16[1,1536,24]{1,2,0:T(8,128)(2,1)S(1)}, bf16[1,1536,24]{1,2,0:T(8,128)(2,1)}, u32[]{:S(2)}) copy-start(bf16[1,1536,24]{1,2,0:T(8,128)(2,1)} %param.13) | copy-start | bytes 221188
  2.3 10.2 %collective-permute-start = (f32[1,128,256]{2,1,0:T(8,128)S(1)}, f32[1,128,256]{2,1,0:T(8,128)S(1)}, u32[]{:S(2)}, u32[]{:S(2)}) collective-permute-start(f32[1,128,256]{2,1,0:T(8,128)S(1)} %bitcast.563), channel_id=1, source_target_pairs={{0,16},{16,0},{1,17},{17,1},{2,18},{18,2},{3,19},{19,3},{4,20},{20... | collective-permute-start | bytes 393224 | tf_op jit(solution)/shard_map/ppermute | solution.py:16
  5.4 18.9 %collective-permute-start.1 = (f32[1,128,256]{2,1,0:T(8,128)S(1)}, f32[1,128,256]{2,1,0:T(8,128)S(1)}, u32[]{:S(2)}, u32[]{:S(2)}) collective-permute-start(f32[1,128,256]{2,1,0:T(8,128)S(1)} %bitcast.564), channel_id=1, source_target_pairs={{16,0},{0,16},{17,1},{1,17},{18,2},{2,18},{19,3},{3,19},{20,4},{4,... | collective-permute-start | bytes 393224 | tf_op jit(solution)/shard_map/ppermute | solution.py:19
  5.6 19.7 %collective-permute-start.2 = (f32[1,128,256]{2,1,0:T(8,128)S(1)}, f32[1,128,256]{2,1,0:T(8,128)S(1)}, u32[]{:S(2)}, u32[]{:S(2)}) collective-permute-start(f32[1,128,256]{2,1,0:T(8,128)S(1)} %bitcast.560), channel_id=1, source_target_pairs={{0,1},{1,2},{2,3},{3,4},{4,5},{5,6},{6,7},{7,8},{8,9},{9,10},{10,1... | collective-permute-start | bytes 393224 | tf_op jit(solution)/shard_map/ppermute | solution.py:16
  5.8 20.5 %collective-permute-start.3 = (f32[1,128,256]{2,1,0:T(8,128)S(1)}, f32[1,128,256]{2,1,0:T(8,128)S(1)}, u32[]{:S(2)}, u32[]{:S(2)}) collective-permute-start(f32[1,128,256]{2,1,0:T(8,128)S(1)} %bitcast.561), channel_id=1, source_target_pairs={{1,0},{2,1},{3,2},{4,3},{5,4},{6,5},{7,6},{8,7},{9,8},{10,9},{11,1... | collective-permute-start | bytes 393224 | tf_op jit(solution)/shard_map/ppermute | solution.py:19
  10.4 16.9 %collective-permute-start.4 = (f32[128,256]{1,0:T(8,128)S(1)}, f32[128,256]{1,0:T(8,128)S(1)}, u32[]{:S(2)}, u32[]{:S(2)}) collective-permute-start(f32[128,256]{1,0:T(8,128)S(1)} %bitcast.559), channel_id=1, source_target_pairs={{0,4},{1,5},{2,6},{3,7},{4,8},{5,9},{6,10},{7,11},{8,12},{9,13},{1... | collective-permute-start | bytes 393224 | tf_op jit(solution)/shard_map/ppermute | solution.py:27
  11.5 41.2 %copy-start.70 = (pred[256]{0:T(512)(128)(4,1)}, pred[256]{0:T(512)(128)(4,1)S(1)}, u32[]{:S(2)}) copy-start(pred[256]{0:T(512)(128)(4,1)S(1)} %compare_and_fusion.5) | copy-start | bytes 772
  11.5 45.2 %copy-start.68 = (pred[256]{0:T(512)(128)(4,1)}, pred[256]{0:T(512)(128)(4,1)S(1)}, u32[]{:S(2)}) copy-start(pred[256]{0:T(512)(128)(4,1)S(1)} %compare_and_fusion.4) | copy-start | bytes 772
  11.6 45.8 %copy-start.66 = (pred[256]{0:T(512)(128)(4,1)}, pred[256]{0:T(512)(128)(4,1)S(1)}, u32[]{:S(2)}) copy-start(pred[256]{0:T(512)(128)(4,1)S(1)} %compare_and_fusion.3) | copy-start | bytes 772
  11.6 46.5 %copy-start.64 = (pred[256]{0:T(512)(128)(4,1)}, pred[256]{0:T(512)(128)(4,1)S(1)}, u32[]{:S(2)}) copy-start(pred[256]{0:T(512)(128)(4,1)S(1)} %compare_and_fusion.2) | copy-start | bytes 772
  11.6 47.0 %copy-start.62 = (pred[256]{0:T(512)(128)(4,1)}, pred[256]{0:T(512)(128)(4,1)S(1)}, u32[]{:S(2)}) copy-start(pred[256]{0:T(512)(128)(4,1)S(1)} %compare_and_fusion.1) | copy-start | bytes 772
  11.7 47.7 %copy-start.60 = (pred[256]{0:T(512)(128)(4,1)}, pred[256]{0:T(512)(128)(4,1)S(1)}, u32[]{:S(2)}) copy-start(pred[256]{0:T(512)(128)(4,1)S(1)} %compare_and_fusion) | copy-start | bytes 772
  12.5 15.7 %collective-permute-start.5 = (f32[128,256]{1,0:T(8,128)S(1)}, f32[128,256]{1,0:T(8,128)S(1)}, u32[]{:S(2)}, u32[]{:S(2)}) collective-permute-start(f32[128,256]{1,0:T(8,128)S(1)} %bitcast.562), channel_id=1, source_target_pairs={{0,12},{1,13},{2,14},{3,15},{4,0},{5,1},{6,2},{7,3},{8,4},{9,5},{1... | collective-permute-start | bytes 393224 | tf_op jit(solution)/shard_map/ppermute | solution.py:27
  37.3 6.8 %collective-permute-start.6 = (f32[1,128,256]{2,1,0:T(8,128)S(1)}, f32[1,128,256]{2,1,0:T(8,128)S(1)}, u32[]{:S(2)}, u32[]{:S(2)}) collective-permute-start(f32[1,128,256]{2,1,0:T(8,128)S(1)} %get-tuple-element.33), channel_id=1, source_target_pairs={{0,16},{16,0},{1,17},{17,1},{2,18},{18,2},{3,19},{19,3},{4,20},{20... | collective-permute-start | bytes 393224 | tf_op jit(solution)/shard_map/ppermute | solution.py:16
  39.3 9.5 %collective-permute-start.7 = (f32[1,128,256]{2,1,0:T(8,128)S(1)}, f32[1,128,256]{2,1,0:T(8,128)S(1)}, u32[]{:S(2)}, u32[]{:S(2)}) collective-permute-start(f32[1,128,256]{2,1,0:T(8,128)S(1)} %get-tuple-element.29), channel_id=1, source_target_pairs={{16,0},{0,16},{17,1},{1,17},{18,2},{2,18},{19,3},{3,19},{20,4},{4,... | collective-permute-start | bytes 393224 | tf_op jit(solution)/shard_map/ppermute | solution.py:19
  39.4 10.4 %collective-permute-start.8 = (f32[1,128,256]{2,1,0:T(8,128)S(1)}, f32[1,128,256]{2,1,0:T(8,128)S(1)}, u32[]{:S(2)}, u32[]{:S(2)}) collective-permute-start(f32[1,128,256]{2,1,0:T(8,128)S(1)} %get-tuple-element.32), channel_id=1, source_target_pairs={{0,1},{1,2},{2,3},{3,4},{4,5},{5,6},{6,7},{7,8},{8,9},{9,10},{10,1... | collective-permute-start | bytes 393224 | tf_op jit(solution)/shard_map/ppermute | solution.py:16
  39.4 11.3 %collective-permute-start.9 = (f32[1,128,256]{2,1,0:T(8,128)S(1)}, f32[1,128,256]{2,1,0:T(8,128)S(1)}, u32[]{:S(2)}, u32[]{:S(2)}) collective-permute-start(f32[1,128,256]{2,1,0:T(8,128)S(1)} %get-tuple-element.30), channel_id=1, source_target_pairs={{1,0},{2,1},{3,2},{4,3},{5,4},{6,5},{7,6},{8,7},{9,8},{10,9},{11,1... | collective-permute-start | bytes 393224 | tf_op jit(solution)/shard_map/ppermute | solution.py:19
  43.9 7.8 %collective-permute-start.10 = (f32[128,256]{1,0:T(8,128)S(1)}, f32[128,256]{1,0:T(8,128)S(1)}, u32[]{:S(2)}, u32[]{:S(2)}) collective-permute-start(f32[128,256]{1,0:T(8,128)S(1)} %get-tuple-element.31), channel_id=1, source_target_pairs={{0,4},{1,5},{2,6},{3,7},{4,8},{5,9},{6,10},{7,11},{8,12},{9,13},{1... | collective-permute-start | bytes 393224 | tf_op jit(solution)/shard_map/ppermute | solution.py:27
  44.0 9.3 %collective-permute-start.11 = (f32[128,256]{1,0:T(8,128)S(1)}, f32[128,256]{1,0:T(8,128)}, u32[]{:S(2)}, u32[]{:S(2)}) collective-permute-start(f32[128,256]{1,0:T(8,128)S(1)} %get-tuple-element.28), channel_id=1, source_target_pairs={{0,12},{1,13},{2,14},{3,15},{4,0},{5,1},{6,2},{7,3},{8,4},{9,5},{1... | collective-permute-start | bytes 393224 | tf_op jit(solution)/shard_map/ppermute | solution.py:27
  151.1 40.2 %copy-start.39 = (f32[128,1,256]{2,0,1:T(8,128)}, f32[128,1,256]{2,0,1:T(8,128)S(1)}, u32[]{:S(2)}) copy-start(f32[128,1,256]{2,0,1:T(8,128)S(1)} %copy.243) | copy-start | bytes 393220
  151.1 11.0 %collective-permute-start.12 = (f32[1,128,256]{2,1,0:T(8,128)S(1)}, f32[1,128,256]{2,1,0:T(8,128)S(1)}, u32[]{:S(2)}, u32[]{:S(2)}) collective-permute-start(f32[1,128,256]{2,1,0:T(8,128)S(1)} %bitcast.569), channel_id=1, source_target_pairs={{0,16},{16,0},{1,17},{17,1},{2,18},{18,2},{3,19},{19,3},{4,20},{20... | collective-permute-start | bytes 393224 | tf_op jit(solution)/shard_map/ppermute | solution.py:16
  152.3 30.9 %copy-start.44 = (f32[128,1,256]{2,0,1:T(8,128)}, f32[128,1,256]{2,0,1:T(8,128)S(1)}, u32[]{:S(2)}) copy-start(f32[128,1,256]{2,0,1:T(8,128)S(1)} %copy.242) | copy-start | bytes 393220
  152.3 17.9 %collective-permute-start.13 = (f32[1,128,256]{2,1,0:T(8,128)S(1)}, f32[1,128,256]{2,1,0:T(8,128)}, u32[]{:S(2)}, u32[]{:S(2)}) collective-permute-start(f32[1,128,256]{2,1,0:T(8,128)S(1)} %bitcast.570), channel_id=1, source_target_pairs={{16,0},{0,16},{17,1},{1,17},{18,2},{2,18},{19,3},{3,19},{20,4},{4,... | collective-permute-start | bytes 393224 | tf_op jit(solution)/shard_map/ppermute | solution.py:19
  155.3 40.4 %copy-start.37 = (f32[128,1,256]{2,0,1:T(8,128)}, f32[128,1,256]{2,0,1:T(8,128)S(1)}, u32[]{:S(2)}) copy-start(f32[128,1,256]{2,0,1:T(8,128)S(1)} %copy.245) | copy-start | bytes 393220
  155.3 30.3 %copy-start.71 = (pred[256]{0:T(512)(128)(4,1)S(1)}, pred[256]{0:T(512)(128)(4,1)}, u32[]{:S(2)}) copy-start(pred[256]{0:T(512)(128)(4,1)} %copy-done.70) | copy-start | bytes 772
  155.3 18.9 %collective-permute-start.14 = (f32[1,128,256]{2,1,0:T(8,128)S(1)}, f32[1,128,256]{2,1,0:T(8,128)}, u32[]{:S(2)}, u32[]{:S(2)}) collective-permute-start(f32[1,128,256]{2,1,0:T(8,128)S(1)} %bitcast.567), channel_id=1, source_target_pairs={{0,1},{1,2},{2,3},{3,4},{4,5},{5,6},{6,7},{7,8},{8,9},{9,10},{10,1... | collective-permute-start | bytes 393224 | tf_op jit(solution)/shard_map/ppermute | solution.py:16
  155.5 38.0 %copy-start.38 = (f32[128,1,256]{2,0,1:T(8,128)}, f32[128,1,256]{2,0,1:T(8,128)S(1)}, u32[]{:S(2)}) copy-start(f32[128,1,256]{2,0,1:T(8,128)S(1)} %copy.244) | copy-start | bytes 393220
  155.5 22.7 %collective-permute-start.15 = (f32[1,128,256]{2,1,0:T(8,128)S(1)}, f32[1,128,256]{2,1,0:T(8,128)}, u32[]{:S(2)}, u32[]{:S(2)}) collective-permute-start(f32[1,128,256]{2,1,0:T(8,128)S(1)} %bitcast.568), channel_id=1, source_target_pairs={{1,0},{2,1},{3,2},{4,3},{5,4},{6,5},{7,6},{8,7},{9,8},{10,9},{11,1... | collective-permute-start | bytes 393224 | tf_op jit(solution)/shard_map/ppermute | solution.py:19
  161.0 38.2 %copy-start.31 = (f32[128,1,256]{2,0,1:T(8,128)}, f32[128,1,256]{2,0,1:T(8,128)S(1)}, u32[]{:S(2)}) copy-start(f32[128,1,256]{2,0,1:T(8,128)S(1)} %copy.247) | copy-start | bytes 393220
  161.0 21.3 %collective-permute-start.16 = (f32[128,256]{1,0:T(8,128)S(1)}, f32[128,256]{1,0:T(8,128)}, u32[]{:S(2)}, u32[]{:S(2)}) collective-permute-start(f32[128,256]{1,0:T(8,128)S(1)} %bitcast.565), channel_id=1, source_target_pairs={{0,4},{1,5},{2,6},{3,7},{4,8},{5,9},{6,10},{7,11},{8,12},{9,13},{1... | collective-permute-start | bytes 393224 | tf_op jit(solution)/shard_map/ppermute | solution.py:27
  162.1 35.8 %copy-start.33 = (f32[128,1,256]{2,0,1:T(8,128)}, f32[128,1,256]{2,0,1:T(8,128)S(1)}, u32[]{:S(2)}) copy-start(f32[128,1,256]{2,0,1:T(8,128)S(1)} %copy.246) | copy-start | bytes 393220
  162.1 25.8 %collective-permute-start.17 = (f32[128,256]{1,0:T(8,128)S(1)}, f32[128,256]{1,0:T(8,128)}, u32[]{:S(2)}, u32[]{:S(2)}) collective-permute-start(f32[128,256]{1,0:T(8,128)S(1)} %bitcast.566), channel_id=1, source_target_pairs={{0,12},{1,13},{2,14},{3,15},{4,0},{5,1},{6,2},{7,3},{8,4},{9,5},{1... | collective-permute-start | bytes 393224 | tf_op jit(solution)/shard_map/ppermute | solution.py:27
  205.7 6.5 %collective-permute-start.18 = (f32[1,128,256]{2,1,0:T(8,128)S(1)}, f32[1,128,256]{2,1,0:T(8,128)S(1)}, u32[]{:S(2)}, u32[]{:S(2)}) collective-permute-start(f32[1,128,256]{2,1,0:T(8,128)S(1)} %get-tuple-element.21), channel_id=1, source_target_pairs={{0,16},{16,0},{1,17},{17,1},{2,18},{18,2},{3,19},{19,3},{4,20},{20... | collective-permute-start | bytes 393224 | tf_op jit(solution)/shard_map/ppermute | solution.py:16
  205.8 14.2 %collective-permute-start.19 = (f32[1,128,256]{2,1,0:T(8,128)}, f32[1,128,256]{2,1,0:T(8,128)}, u32[]{:S(2)}, u32[]{:S(2)}) collective-permute-start(f32[1,128,256]{2,1,0:T(8,128)} %get-tuple-element.17), channel_id=1, source_target_pairs={{16,0},{0,16},{17,1},{1,17},{18,2},{2,18},{19,3},{3,19},{20,4},{4,... | collective-permute-start | bytes 393224 | tf_op jit(solution)/shard_map/ppermute | solution.py:19
  207.7 16.3 %collective-permute-start.20 = (f32[1,128,256]{2,1,0:T(8,128)}, f32[1,128,256]{2,1,0:T(8,128)}, u32[]{:S(2)}, u32[]{:S(2)}) collective-permute-start(f32[1,128,256]{2,1,0:T(8,128)} %get-tuple-element.20), channel_id=1, source_target_pairs={{0,1},{1,2},{2,3},{3,4},{4,5},{5,6},{6,7},{7,8},{8,9},{9,10},{10,1... | collective-permute-start | bytes 393224 | tf_op jit(solution)/shard_map/ppermute | solution.py:16
  207.7 20.3 %collective-permute-start.21 = (f32[1,128,256]{2,1,0:T(8,128)}, f32[1,128,256]{2,1,0:T(8,128)}, u32[]{:S(2)}, u32[]{:S(2)}) collective-permute-start(f32[1,128,256]{2,1,0:T(8,128)} %get-tuple-element.18), channel_id=1, source_target_pairs={{1,0},{2,1},{3,2},{4,3},{5,4},{6,5},{7,6},{8,7},{9,8},{10,9},{11,1... | collective-permute-start | bytes 393224 | tf_op jit(solution)/shard_map/ppermute | solution.py:19
  212.2 19.9 %collective-permute-start.22 = (f32[128,256]{1,0:T(8,128)}, f32[128,256]{1,0:T(8,128)}, u32[]{:S(2)}, u32[]{:S(2)}) collective-permute-start(f32[128,256]{1,0:T(8,128)} %get-tuple-element.19), channel_id=1, source_target_pairs={{0,4},{1,5},{2,6},{3,7},{4,8},{5,9},{6,10},{7,11},{8,12},{9,13},{1... | collective-permute-start | bytes 393224 | tf_op jit(solution)/shard_map/ppermute | solution.py:27
  212.2 26.1 %collective-permute-start.23 = (f32[128,256]{1,0:T(8,128)}, f32[128,256]{1,0:T(8,128)}, u32[]{:S(2)}, u32[]{:S(2)}) collective-permute-start(f32[128,256]{1,0:T(8,128)} %get-tuple-element.16), channel_id=1, source_target_pairs={{0,12},{1,13},{2,14},{3,15},{4,0},{5,1},{6,2},{7,3},{8,4},{9,5},{1... | collective-permute-start | bytes 393224 | tf_op jit(solution)/shard_map/ppermute | solution.py:27
  241.6 50.7 %copy-start.46 = (f32[256,128]{0,1:T(8,128)}, f32[256,128]{0,1:T(8,128)S(1)}, u32[]{:S(2)}) copy-start(f32[256,128]{0,1:T(8,128)S(1)} %copy.216) | copy-start | bytes 393220
  253.5 85.2 %copy-start.72 = (f32[3,96]{1,0:T(4,128)S(1)}, f32[3,96]{1,0:T(4,128)}, u32[]{:S(2)}) copy-start(f32[3,96]{1,0:T(4,128)} %param.14) | copy-start | bytes 3460
  296.7 103.6 %copy-start.14 = (f32[128,1,256]{2,0,1:T(8,128)S(1)}, f32[128,1,256]{2,0,1:T(8,128)}, u32[]{:S(2)}) copy-start(f32[128,1,256]{2,0,1:T(8,128)} %copy-done.13) | copy-start | bytes 393220
  338.8 56.0 %copy-start.79 = (f32[128]{0:T(128)S(1)}, f32[128]{0:T(128)}, u32[]{:S(2)}) copy-start(f32[128]{0:T(128)} %get-tuple-element.5) | copy-start | bytes 1540
  383.2 12.3 %collective-permute-start.24 = (f32[1,128,256]{2,1,0:T(8,128)S(1)}, f32[1,128,256]{2,1,0:T(8,128)S(1)}, u32[]{:S(2)}, u32[]{:S(2)}) collective-permute-start(f32[1,128,256]{2,1,0:T(8,128)S(1)} %bitcast.574), channel_id=1, source_target_pairs={{0,16},{16,0},{1,17},{17,1},{2,18},{18,2},{3,19},{19,3},{4,20},{20... | collective-permute-start | bytes 393224 | tf_op jit(solution)/shard_map/ppermute | solution.py:16
  384.5 17.3 %collective-permute-start.25 = (f32[1,128,256]{2,1,0:T(8,128)S(1)}, f32[1,128,256]{2,1,0:T(8,128)}, u32[]{:S(2)}, u32[]{:S(2)}) collective-permute-start(f32[1,128,256]{2,1,0:T(8,128)S(1)} %bitcast.575), channel_id=1, source_target_pairs={{16,0},{0,16},{17,1},{1,17},{18,2},{2,18},{19,3},{3,19},{20,4},{4,... | collective-permute-start | bytes 393224 | tf_op jit(solution)/shard_map/ppermute | solution.py:19
  387.4 17.0 %collective-permute-start.26 = (f32[1,128,256]{2,1,0:T(8,128)S(1)}, f32[1,128,256]{2,1,0:T(8,128)}, u32[]{:S(2)}, u32[]{:S(2)}) collective-permute-start(f32[1,128,256]{2,1,0:T(8,128)S(1)} %bitcast.572), channel_id=1, source_target_pairs={{0,1},{1,2},{2,3},{3,4},{4,5},{5,6},{6,7},{7,8},{8,9},{9,10},{10,1... | collective-permute-start | bytes 393224 | tf_op jit(solution)/shard_map/ppermute | solution.py:16
  388.5 18.4 %collective-permute-start.27 = (f32[1,128,256]{2,1,0:T(8,128)S(1)}, f32[1,128,256]{2,1,0:T(8,128)}, u32[]{:S(2)}, u32[]{:S(2)}) collective-permute-start(f32[1,128,256]{2,1,0:T(8,128)S(1)} %bitcast.573), channel_id=1, source_target_pairs={{1,0},{2,1},{3,2},{4,3},{5,4},{6,5},{7,6},{8,7},{9,8},{10,9},{11,1... | collective-permute-start | bytes 393224 | tf_op jit(solution)/shard_map/ppermute | solution.py:19
  394.0 15.5 %collective-permute-start.28 = (f32[128,256]{1,0:T(8,128)S(1)}, f32[128,256]{1,0:T(8,128)}, u32[]{:S(2)}, u32[]{:S(2)}) collective-permute-start(f32[128,256]{1,0:T(8,128)S(1)} %bitcast.571), channel_id=1, source_target_pairs={{0,4},{1,5},{2,6},{3,7},{4,8},{5,9},{6,10},{7,11},{8,12},{9,13},{1... | collective-permute-start | bytes 393224 | tf_op jit(solution)/shard_map/ppermute | solution.py:27
  395.5 16.5 %collective-permute-start.29 = (f32[128,256]{1,0:T(8,128)}, f32[128,256]{1,0:T(8,128)}, u32[]{:S(2)}, u32[]{:S(2)}) collective-permute-start(f32[128,256]{1,0:T(8,128)} %bitcast.155), channel_id=1, source_target_pairs={{0,12},{1,13},{2,14},{3,15},{4,0},{5,1},{6,2},{7,3},{8,4},{9,5},{1... | collective-permute-start | bytes 393224 | tf_op jit(solution)/shard_map/ppermute | solution.py:27
  (63 other events, 895.0 us)
where the time goes:
time: 434 us; the launch traced here: 432 us
  blocking collectives  199 us (46%)
  local copies, waits for them, and re-layouts  101 us (23%)
  starting transfers between devices  53.7 us (12%)
  other arithmetic  53 us (12%)
  matrix products  23.3 us (5%)
    all_gather x2, blocking collectives, local(): lax.all_gather(own_values, ('cluster', 'sub'), axis=1, tiled=True)  82.9 us
    psum x2, blocking collectives, local(): lax.psum((coarse_local, local_curve), ('cluster', 'sub'))  79.2 us
    gather x60, local copies, waits for them, and re-layouts, assemble(): permuted = jnp.take(received[face_index], slot_maps[face_index], axis=1)  55.5 us
    unnamed x25, other arithmetic  39.7 us
    psum x1, blocking collectives, precond_with_product(): lax.psum(jnp.sum(vector * precond, axis=1), ('cluster', 'sub'))  36.9 us
    ppermute x10, starting transfers between devices, padded(): lax.ppermute(lax.slice_in_dim(block, 0, width, axis=dim), axis, backward)  28.2 us
    unnamed x184, local copies, waits for them, and re-layouts  20.4 us
    ppermute x10, starting transfers between devices, passed_along(): return lax.ppermute(value, axis, pairs)  19.6 us
  transfers between devices with their start and end apart: 30, of which 0 were waited for; matrix products, arithmetic and copies ran while one was open for 20% of the time, Pallas kernels for 0%

commit v1 on v0

--- a/solution.py
+++ b/solution.py
@@ -1,3 +1,4 @@
+import functools
 import jax
 import jax.numpy as jnp
 from jax import lax
@@ -5,6 +6,23 @@
 
 ITERS = 2
 STRIDE = 4
+
+
+def _pack_things(u, at_axis):
+    local_part, newest = (lax.axis_size(("cluster", "sub")), lax.axis_index(("cluster", "sub")))
+    last, big = (u, 1)
+    while big < local_part:
+        wide_out = lax.ppermute(
+            last, ("cluster", "sub"), tuple(((ix, ix ^ big) for ix in range(local_part)))
+        )
+        block_last = jnp.concatenate([last, wide_out], axis=at_axis)
+        everything = jnp.concatenate([wide_out, last], axis=at_axis)
+        last = jnp.where(newest & big == 0, block_last, everything)
+        big = 2 * big
+    return last
+
+
+register_the_stocks = functools.partial(_pack_things, at_axis=1)
 
 
 def padded(block, sides, width):
@@ -95,7 +113,7 @@
         local_curve = jnp.sum(direction * direct, axis=1)
         apply_coarse_load, curve_total = lax.psum((coarse_local, local_curve), ("cluster", "sub"))
         own_values = jnp.dot(apply_coarse_load, coarse_inverse.T, precision=lax.Precision.HIGHEST)
-        solution = lax.all_gather(own_values, ("cluster", "sub"), axis=1, tiled=True)
+        solution = register_the_stocks(own_values)
         corner_values = jnp.dot(solution, spread.T, precision=lax.Precision.HIGHEST).astype(
             jnp.bfloat16
         )

time: 434 us -> 390 us (0.90)
  blocking collectives: 199 us -> 118 us
  waiting for transfers between devices: 0.08 us -> 21.3 us
  starting transfers between devices: 53.7 us -> 67.9 us
    all_gather x2 -> x0, blocking collectives: 82.9 us -> none  [local(): lax.all_gather(own_values, ('cluster', 'sub'), axis=1, tiled=True)]
    ppermute x0 -> x10, waiting for transfers between devices: none -> 21.3 us  [_pack_things(): lax.ppermute(last, ('cluster', 'sub'), tuple(((ix, ix ^ big) for ix in ra...]
    ppermute x0 -> x10, starting transfers between devices: none -> 14.1 us  [_pack_things(): lax.ppermute(last, ('cluster', 'sub'), tuple(((ix, ix ^ big) for ix in ra...]
    ppermute x10, starting transfers between devices: 28.2 us -> 22.6 us  [padded(): lax.ppermute(lax.slice_in_dim(block, 0, width, axis=dim), axis, backward)]
    ppermute x10, starting transfers between devices: 5.88 us -> 11.4 us  [padded(): lax.ppermute(lax.slice_in_dim(block, block.shape[dim] - width, None, axis...]
    unnamed x184 -> x212, local copies, waits for them, and re-layouts: 20.4 us -> 19.9 us
  transfers between devices with their start and end apart: 30 -> 40, of which waited for: 0 -> 10; matrix products, arithmetic and copies ran while one was open for 20% -> 23% of each run, Pallas kernels for 0% -> 0%
where the time goes in v1:
time: 390 us; the launch traced here: 388 us
  blocking collectives  118 us (30%)
  local copies, waits for them, and re-layouts  101 us (26%)
  starting transfers between devices  67.9 us (17%)
  other arithmetic  54 us (14%)
  matrix products  22.2 us (6%)
  waiting for transfers between devices  21.3 us (5%)
    psum x2, blocking collectives, local(): lax.psum((coarse_local, local_curve), ('cluster', 'sub'))  81 us
    gather x60, local copies, waits for them, and re-layouts, assemble(): permuted = jnp.take(received[face_index], slot_maps[face_index], axis=1)  54.7 us
    unnamed x25, other arithmetic  39.6 us
    psum x1, blocking collectives, precond_with_product(): lax.psum(jnp.sum(vector * precond, axis=1), ('cluster', 'sub'))  36.9 us
    ppermute x10, starting transfers between devices, padded(): lax.ppermute(lax.slice_in_dim(block, 0, width, axis=dim), axis, backward)  22.6 us
    ppermute x10, waiting for transfers between devices, _pack_things(): lax.ppermute(last, ('cluster', 'sub'), tuple(((ix, ix ^ big) for ix in ra...  21.3 us
    unnamed x212, local copies, waits for them, and re-layouts  19.9 us
    ppermute x10, starting transfers between devices, passed_along(): return lax.ppermute(value, axis, pairs)  19.8 us
  transfers between devices with their start and end apart: 40, of which 10 were waited for; matrix products, arithmetic and copies ran while one was open for 23% of the time, Pallas kernels for 0%

profile of v1, /device:TPU:0, one launch (start us, length us, event | category | flops | bytes accessed | tf_op | source)
XLA Modules:
  0.0 387.6 jit_solution(3260936831795916987)
XLA Ops:
  2.3 3.0 collective-permute-start
  5.8 4.5 %collective-permute-start.3 = (f32[1,128,256]{2,1,0:T(8,128)S(1)}, f32[1,128,256]{2,1,0:T(8,128)S(1)}, u32[]{:S(2)}, u32[]{:S(2)}) collective-permute-start(f32[1,128,256]{2,1,0:T(8,128)S(1)} %bitcast.543), channel_id=1, source_target_pairs={{1,0},{2,1},{3,2},{4,3},{5,4},{6,5},{7,6},{8,7},{9,8},{10,9},{11,1... | collective-permute-start | bytes 393224 | tf_op jit(solution)/shard_map/ppermute | solution.py:37
  12.6 3.6 collective-permute-start.5
  16.2 6.6 %copy.91 = bf16[1,1536,1536]{1,2,0:T(8,128)(2,1)} copy(bf16[1,1536,1536]{2,1,0:T(8,128)(2,1)} %param.12) | data formatting | bytes 9437184 | tf_op args[2]
  33.0 4.0 %fusion.6 = f32[128,6,256]{2,0,1:T(8,128)S(1)} fusion(bf16[6,256,1536]{2,1,0:T(8,128)(2,1)} %bitcast.536, f32[128,1536]{1,0:T(8,128)S(1)} %constant_dynamic-update-slice_fusion), kind=kOutput, calls=%fused_computation.48 | convolution fusion | flops 604176384 | bytes 6291456 | tf_op jit(solution)/shard_map/dot_general | solution.py:96
  37.7 2.0 collective-permute-start.6
  39.7 4.4 %collective-permute-start.9 = (f32[1,128,256]{2,1,0:T(8,128)S(1)}, f32[1,128,256]{2,1,0:T(8,128)S(1)}, u32[]{:S(2)}, u32[]{:S(2)}) collective-permute-start(f32[1,128,256]{2,1,0:T(8,128)S(1)} %get-tuple-element.30), channel_id=1, source_target_pairs={{1,0},{2,1},{3,2},{4,3},{5,4},{6,5},{7,6},{8,7},{9,8},{10,9},{11,1... | collective-permute-start | bytes 393224 | tf_op jit(solution)/shard_map/ppermute | solution.py:37
  44.9 3.8 collective-permute-start.11
  59.1 3.8 multiply_reduce_fusion.3
  63.5 37.7 %all-reduce.1 = (f32[128,96]{0,1:T(8,128)S(1)}, f32[128]{0:T(128)}, f32[128]{0:T(128)}) all-reduce(f32[128,96]{0,1:T(8,128)S(1)} %fusion.53, f32[128]{0:T(128)} %get-tuple-element.4, f32[128]{0:T(128)} %get-tuple-element.3), channel_id=1, replica_groups=mesh['cluster'=2,'sub'=16] {'cluster','sub'}, use_global_device_ids=true, to_apply=%region_4.6 | all-reduce | flops 12544 | bytes 100352 | tf_op jit(solution)/shard_map/psum | solution.py:114
  103.2 2.3 collective-permute-start.13
  107.1 2.8 collective-permute-start.14
  111.6 2.3 collective-permute-start.15
  114.0 2.3 collective-permute-done.15
  116.3 2.0 collective-permute-start.16
  118.3 1.8 collective-permute-done.16
  125.4 2.1 collective-permute-start.17
  129.8 4.5 %collective-permute-start.20 = (f32[1,128,256]{2,1,0:T(8,128)S(1)}, f32[1,128,256]{2,1,0:T(8,128)}, u32[]{:S(2)}, u32[]{:S(2)}) collective-permute-start(f32[1,128,256]{2,1,0:T(8,128)S(1)} %bitcast.550), channel_id=1, source_target_pairs={{1,0},{2,1},{3,2},{4,3},{5,4},{6,5},{7,6},{8,7},{9,8},{10,9},{11,1... | collective-permute-start | bytes 393224 | tf_op jit(solution)/shard_map/ppermute | solution.py:37
  138.1 3.8 collective-permute-start.22
  161.4 2.2 constant_dynamic-update-slice_fusion.17
  167.0 2.2 constant_dynamic-update-slice_fusion.16
  169.1 2.1 constant_dynamic-update-slice_fusion.15
  171.3 2.2 constant_dynamic-update-slice_fusion.14
  176.0 4.3 %fusion.4 = f32[128,6,256]{2,0,1:T(8,128)S(1)} fusion(bf16[6,256,1536]{2,1,0:T(8,128)(2,1)} %bitcast.537, f32[128,1536]{1,0:T(8,128)S(1)} %constant_dynamic-update-slice_fusion, f32[128,1536]{1,0:T(8,128)} %constant_dynamic-update-slice_fusion.12, f32[128]{0:T(128)S(1)} %add_divide_fusion.1), kind=kOutput, calls=%fused_computation.46 | convolution fusion | flops 604569600 | bytes 7078400 | tf_op jit(solution)/shard_map/dot_general | solution.py:96
  181.1 2.0 collective-permute-start.23
  183.2 4.4 %collective-permute-start.26 = (f32[1,128,256]{2,1,0:T(8,128)}, f32[1,128,256]{2,1,0:T(8,128)}, u32[]{:S(2)}, u32[]{:S(2)}) collective-permute-start(f32[1,128,256]{2,1,0:T(8,128)} %get-tuple-element.18), channel_id=1, source_target_pairs={{1,0},{2,1},{3,2},{4,3},{5,4},{6,5},{7,6},{8,7},{9,8},{10,9},{11,1... | collective-permute-start | bytes 393224 | tf_op jit(solution)/shard_map/ppermute | solution.py:37
  187.6 3.8 collective-permute-start.28
  211.5 2.2 constant_dynamic-update-slice_fusion.23
  217.0 2.2 constant_dynamic-update-slice_fusion.22
  219.2 2.1 constant_dynamic-update-slice_fusion.21
  221.4 2.2 constant_dynamic-update-slice_fusion.20
  223.6 2.2 constant_dynamic-update-slice_fusion.19
  228.7 36.9 %psum.45 = f32[128]{0:T(128)S(1)} all-reduce(f32[128]{0:T(128)S(1)} %multiply_reduce_fusion.1), channel_id=1, replica_groups=mesh['cluster'=2,'sub'=16] {'cluster','sub'}, use_global_device_ids=true, to_apply=%region_7.9 | all-reduce | flops 128 | bytes 1024 | tf_op jit(solution)/shard_map/psum | solution.py:100
  267.1 3.8 multiply_reduce_fusion
  271.2 43.3 %all-reduce = (f32[128]{0:T(128)}, f32[128,96]{0,1:T(8,128)S(1)}) all-reduce(f32[128]{0:T(128)S(1)} %get-tuple-element.85, f32[128,96]{0,1:T(8,128)S(1)} %fusion.52), channel_id=1, replica_groups=mesh['cluster'=2,'sub'=16] {'cluster','sub'}, use_global_device_ids=true, to_apply=%region_9.11 | all-reduce | flops 12416 | bytes 99328 | tf_op jit(solution)/shard_map/psum | solution.py:114
  315.9 2.3 collective-permute-start.30
  319.9 3.6 collective-permute-done.31
  323.7 4.5 %collective-permute-done.32 = f32[128,24]{0,1:T(8,128)S(1)} collective-permute-done((f32[128,24]{0,1:T(8,128)S(1)}, f32[128,24]{0,1:T(8,128)S(1)}, u32[]{:S(2)}, u32[]{:S(2)}) %collective-permute-start.32) | collective-permute-done | bytes 12320 | tf_op jit(solution)/shard_map/ppermute | solution.py:15
  328.2 2.0 collective-permute-start.33
  335.4 2.1 collective-permute-start.34
  340.6 4.5 %collective-permute-start.37 = (f32[1,128,256]{2,1,0:T(8,128)S(1)}, f32[1,128,256]{2,1,0:T(8,128)}, u32[]{:S(2)}, u32[]{:S(2)}) collective-permute-start(f32[1,128,256]{2,1,0:T(8,128)S(1)} %bitcast.555), channel_id=1, source_target_pairs={{1,0},{2,1},{3,2},{4,3},{5,4},{6,5},{7,6},{8,7},{9,8},{10,9},{11,1... | collective-permute-start | bytes 393224 | tf_op jit(solution)/shard_map/ppermute | solution.py:37
  348.4 4.1 %collective-permute-start.39 = (f32[128,256]{1,0:T(8,128)}, f32[128,256]{1,0:T(8,128)}, u32[]{:S(2)}, u32[]{:S(2)}) collective-permute-start(f32[128,256]{1,0:T(8,128)} %bitcast.149), channel_id=1, source_target_pairs={{0,12},{1,13},{2,14},{3,15},{4,0},{5,1},{6,2},{7,3},{8,4},{9,5},{1... | collective-permute-start | bytes 393224 | tf_op jit(solution)/shard_map/ppermute | solution.py:45
  354.5 2.1 bitcast_dynamic-update-slice_fusion.11
  371.8 2.8 bitcast_dynamic-update-slice_fusion.10
  374.6 2.6 bitcast_dynamic-update-slice_fusion.9
  377.2 2.7 bitcast_dynamic-update-slice_fusion.8
  380.0 2.4 bitcast_dynamic-update-slice_fusion.7
  383.9 3.8 multiply_subtract_fusion
  (427 shorter events, 129.7 us)
Async XLA Ops:
  2.3 10.3 %collective-permute-start = (f32[1,128,256]{2,1,0:T(8,128)S(1)}, f32[1,128,256]{2,1,0:T(8,128)S(1)}, u32[]{:S(2)}, u32[]{:S(2)}) collective-permute-start(f32[1,128,256]{2,1,0:T(8,128)S(1)} %bitcast.545), channel_id=1, source_target_pairs={{0,16},{16,0},{1,17},{17,1},{2,18},{18,2},{3,19},{19,3},{4,20},{20... | collective-permute-start | bytes 393224 | tf_op jit(solution)/shard_map/ppermute | solution.py:34
  5.4 19.0 %collective-permute-start.1 = (f32[1,128,256]{2,1,0:T(8,128)S(1)}, f32[1,128,256]{2,1,0:T(8,128)S(1)}, u32[]{:S(2)}, u32[]{:S(2)}) collective-permute-start(f32[1,128,256]{2,1,0:T(8,128)S(1)} %bitcast.546), channel_id=1, source_target_pairs={{16,0},{0,16},{17,1},{1,17},{18,2},{2,18},{19,3},{3,19},{20,4},{4,... | collective-permute-start | bytes 393224 | tf_op jit(solution)/shard_map/ppermute | solution.py:37
  5.6 19.7 %collective-permute-start.2 = (f32[1,128,256]{2,1,0:T(8,128)S(1)}, f32[1,128,256]{2,1,0:T(8,128)S(1)}, u32[]{:S(2)}, u32[]{:S(2)}) collective-permute-start(f32[1,128,256]{2,1,0:T(8,128)S(1)} %bitcast.542), channel_id=1, source_target_pairs={{0,1},{1,2},{2,3},{3,4},{4,5},{5,6},{6,7},{7,8},{8,9},{9,10},{10,1... | collective-permute-start | bytes 393224 | tf_op jit(solution)/shard_map/ppermute | solution.py:34
  5.8 20.5 %collective-permute-start.3 = (f32[1,128,256]{2,1,0:T(8,128)S(1)}, f32[1,128,256]{2,1,0:T(8,128)S(1)}, u32[]{:S(2)}, u32[]{:S(2)}) collective-permute-start(f32[1,128,256]{2,1,0:T(8,128)S(1)} %bitcast.543), channel_id=1, source_target_pairs={{1,0},{2,1},{3,2},{4,3},{5,4},{6,5},{7,6},{8,7},{9,8},{10,9},{11,1... | collective-permute-start | bytes 393224 | tf_op jit(solution)/shard_map/ppermute | solution.py:37
  10.4 16.9 %collective-permute-start.4 = (f32[128,256]{1,0:T(8,128)S(1)}, f32[128,256]{1,0:T(8,128)S(1)}, u32[]{:S(2)}, u32[]{:S(2)}) collective-permute-start(f32[128,256]{1,0:T(8,128)S(1)} %bitcast.541), channel_id=1, source_target_pairs={{0,4},{1,5},{2,6},{3,7},{4,8},{5,9},{6,10},{7,11},{8,12},{9,13},{1... | collective-permute-start | bytes 393224 | tf_op jit(solution)/shard_map/ppermute | solution.py:45
  11.7 180.8 %copy-start.68 = (s32[1024]{0:T(1024)}, s32[1024]{0:T(1024)S(1)}, u32[]{:S(2)}) copy-start(s32[1024]{0:T(1024)S(1)} %pad_clamp_fusion.5) | copy-start | bytes 12292
  11.7 184.7 %copy-start.67 = (s32[1024]{0:T(1024)}, s32[1024]{0:T(1024)S(1)}, u32[]{:S(2)}) copy-start(s32[1024]{0:T(1024)S(1)} %pad_clamp_fusion.4) | copy-start | bytes 12292
  11.7 188.7 %copy-start.66 = (s32[1024]{0:T(1024)}, s32[1024]{0:T(1024)S(1)}, u32[]{:S(2)}) copy-start(s32[1024]{0:T(1024)S(1)} %pad_clamp_fusion.3) | copy-start | bytes 12292
  12.4 192.1 %copy-start.65 = (s32[1024]{0:T(1024)}, s32[1024]{0:T(1024)S(1)}, u32[]{:S(2)}) copy-start(s32[1024]{0:T(1024)S(1)} %pad_clamp_fusion.2) | copy-start | bytes 12292
  12.5 196.0 %copy-start.64 = (s32[1024]{0:T(1024)}, s32[1024]{0:T(1024)S(1)}, u32[]{:S(2)}) copy-start(s32[1024]{0:T(1024)S(1)} %pad_clamp_fusion.1) | copy-start | bytes 12292
  12.6 15.6 %collective-permute-start.5 = (f32[128,256]{1,0:T(8,128)S(1)}, f32[128,256]{1,0:T(8,128)S(1)}, u32[]{:S(2)}, u32[]{:S(2)}) collective-permute-start(f32[128,256]{1,0:T(8,128)S(1)} %bitcast.544), channel_id=1, source_target_pairs={{0,12},{1,13},{2,14},{3,15},{4,0},{5,1},{6,2},{7,3},{8,4},{9,5},{1... | collective-permute-start | bytes 393224 | tf_op jit(solution)/shard_map/ppermute | solution.py:45
  16.2 198.5 %copy-start.63 = (s32[1024]{0:T(1024)}, s32[1024]{0:T(1024)S(1)}, u32[]{:S(2)}) copy-start(s32[1024]{0:T(1024)S(1)} %pad_clamp_fusion) | copy-start | bytes 12292
  37.7 7.2 %collective-permute-start.6 = (f32[1,128,256]{2,1,0:T(8,128)S(1)}, f32[1,128,256]{2,1,0:T(8,128)S(1)}, u32[]{:S(2)}, u32[]{:S(2)}) collective-permute-start(f32[1,128,256]{2,1,0:T(8,128)S(1)} %get-tuple-element.33), channel_id=1, source_target_pairs={{0,16},{16,0},{1,17},{17,1},{2,18},{18,2},{3,19},{19,3},{4,20},{20... | collective-permute-start | bytes 393224 | tf_op jit(solution)/shard_map/ppermute | solution.py:34
  39.7 9.9 %collective-permute-start.7 = (f32[1,128,256]{2,1,0:T(8,128)S(1)}, f32[1,128,256]{2,1,0:T(8,128)S(1)}, u32[]{:S(2)}, u32[]{:S(2)}) collective-permute-start(f32[1,128,256]{2,1,0:T(8,128)S(1)} %get-tuple-element.29), channel_id=1, source_target_pairs={{16,0},{0,16},{17,1},{1,17},{18,2},{2,18},{19,3},{3,19},{20,4},{4,... | collective-permute-start | bytes 393224 | tf_op jit(solution)/shard_map/ppermute | solution.py:37
  39.7 10.9 %collective-permute-start.8 = (f32[1,128,256]{2,1,0:T(8,128)S(1)}, f32[1,128,256]{2,1,0:T(8,128)S(1)}, u32[]{:S(2)}, u32[]{:S(2)}) collective-permute-start(f32[1,128,256]{2,1,0:T(8,128)S(1)} %get-tuple-element.32), channel_id=1, source_target_pairs={{0,1},{1,2},{2,3},{3,4},{4,5},{5,6},{6,7},{7,8},{8,9},{9,10},{10,1... | collective-permute-start | bytes 393224 | tf_op jit(solution)/shard_map/ppermute | solution.py:34
  39.7 11.8 %collective-permute-start.9 = (f32[1,128,256]{2,1,0:T(8,128)S(1)}, f32[1,128,256]{2,1,0:T(8,128)S(1)}, u32[]{:S(2)}, u32[]{:S(2)}) collective-permute-start(f32[1,128,256]{2,1,0:T(8,128)S(1)} %get-tuple-element.30), channel_id=1, source_target_pairs={{1,0},{2,1},{3,2},{4,3},{5,4},{6,5},{7,6},{8,7},{9,8},{10,9},{11,1... | collective-permute-start | bytes 393224 | tf_op jit(solution)/shard_map/ppermute | solution.py:37
  44.2 8.3 %collective-permute-start.10 = (f32[128,256]{1,0:T(8,128)S(1)}, f32[128,256]{1,0:T(8,128)S(1)}, u32[]{:S(2)}, u32[]{:S(2)}) collective-permute-start(f32[128,256]{1,0:T(8,128)S(1)} %get-tuple-element.31), channel_id=1, source_target_pairs={{0,4},{1,5},{2,6},{3,7},{4,8},{5,9},{6,10},{7,11},{8,12},{9,13},{1... | collective-permute-start | bytes 393224 | tf_op jit(solution)/shard_map/ppermute | solution.py:45
  44.9 9.2 %collective-permute-start.11 = (f32[128,256]{1,0:T(8,128)}, f32[128,256]{1,0:T(8,128)}, u32[]{:S(2)}, u32[]{:S(2)}) collective-permute-start(f32[128,256]{1,0:T(8,128)} %get-tuple-element.28), channel_id=1, source_target_pairs={{0,12},{1,13},{2,14},{3,15},{4,0},{5,1},{6,2},{7,3},{8,4},{9,5},{1... | collective-permute-start | bytes 393224 | tf_op jit(solution)/shard_map/ppermute | solution.py:45
  102.0 1.2 collective-permute-start.12
  103.2 3.9 %collective-permute-start.13 = (f32[128,6]{0,1:T(8,128)S(1)}, f32[128,6]{0,1:T(8,128)S(1)}, u32[]{:S(2)}, u32[]{:S(2)}) collective-permute-start(f32[128,6]{0,1:T(8,128)S(1)} %maximum_select_fusion.10), channel_id=1, source_target_pairs={{0,2},{1,3},{2,0},{3,1},{4,6},{5,7},{6,4},{7,5},{8,10},{9,11},{10,... | collective-permute-start | bytes 9224 | tf_op jit(solution)/shard_map/ppermute | solution.py:15
  107.1 4.5 %collective-permute-start.14 = (f32[128,12]{0,1:T(8,128)S(1)}, f32[128,12]{0,1:T(8,128)S(1)}, u32[]{:S(2)}, u32[]{:S(2)}) collective-permute-start(f32[128,12]{0,1:T(8,128)S(1)} %maximum_select_fusion.8), channel_id=1, source_target_pairs={{0,4},{1,5},{2,6},{3,7},{4,0},{5,1},{6,2},{7,3},{8,12},{9,13},{10,... | collective-permute-start | bytes 18440 | tf_op jit(solution)/shard_map/ppermute | solution.py:15
  111.6 4.7 %collective-permute-start.15 = (f32[128,24]{0,1:T(8,128)S(1)}, f32[128,24]{0,1:T(8,128)S(1)}, u32[]{:S(2)}, u32[]{:S(2)}) collective-permute-start(f32[128,24]{0,1:T(8,128)S(1)} %maximum_select_fusion.6), channel_id=1, source_target_pairs={{0,8},{1,9},{2,10},{3,11},{4,12},{5,13},{6,14},{7,15},{8,0},{9,1},... | collective-permute-start | bytes 36872 | tf_op jit(solution)/shard_map/ppermute | solution.py:15
  116.3 3.8 collective-permute-start.16
  125.4 12.7 %collective-permute-start.17 = (f32[1,128,256]{2,1,0:T(8,128)S(1)}, f32[1,128,256]{2,1,0:T(8,128)S(1)}, u32[]{:S(2)}, u32[]{:S(2)}) collective-permute-start(f32[1,128,256]{2,1,0:T(8,128)S(1)} %bitcast.551), channel_id=1, source_target_pairs={{0,16},{16,0},{1,17},{17,1},{2,18},{18,2},{3,19},{19,3},{4,20},{20... | collective-permute-start | bytes 393224 | tf_op jit(solution)/shard_map/ppermute | solution.py:34
  128.5 17.4 %collective-permute-start.18 = (f32[1,128,256]{2,1,0:T(8,128)S(1)}, f32[1,128,256]{2,1,0:T(8,128)}, u32[]{:S(2)}, u32[]{:S(2)}) collective-permute-start(f32[1,128,256]{2,1,0:T(8,128)S(1)} %bitcast.552), channel_id=1, source_target_pairs={{16,0},{0,16},{17,1},{1,17},{18,2},{2,18},{19,3},{3,19},{20,4},{4,... | collective-permute-start | bytes 393224 | tf_op jit(solution)/shard_map/ppermute | solution.py:37
  129.6 20.4 %collective-permute-start.19 = (f32[1,128,256]{2,1,0:T(8,128)S(1)}, f32[1,128,256]{2,1,0:T(8,128)}, u32[]{:S(2)}, u32[]{:S(2)}) collective-permute-start(f32[1,128,256]{2,1,0:T(8,128)S(1)} %bitcast.549), channel_id=1, source_target_pairs={{0,1},{1,2},{2,3},{3,4},{4,5},{5,6},{6,7},{7,8},{8,9},{9,10},{10,1... | collective-permute-start | bytes 393224 | tf_op jit(solution)/shard_map/ppermute | solution.py:34
  129.8 24.2 %collective-permute-start.20 = (f32[1,128,256]{2,1,0:T(8,128)S(1)}, f32[1,128,256]{2,1,0:T(8,128)}, u32[]{:S(2)}, u32[]{:S(2)}) collective-permute-start(f32[1,128,256]{2,1,0:T(8,128)S(1)} %bitcast.550), channel_id=1, source_target_pairs={{1,0},{2,1},{3,2},{4,3},{5,4},{6,5},{7,6},{8,7},{9,8},{10,9},{11,1... | collective-permute-start | bytes 393224 | tf_op jit(solution)/shard_map/ppermute | solution.py:37
  135.3 22.7 %collective-permute-start.21 = (f32[128,256]{1,0:T(8,128)S(1)}, f32[128,256]{1,0:T(8,128)}, u32[]{:S(2)}, u32[]{:S(2)}) collective-permute-start(f32[128,256]{1,0:T(8,128)S(1)} %bitcast.547), channel_id=1, source_target_pairs={{0,4},{1,5},{2,6},{3,7},{4,8},{5,9},{6,10},{7,11},{8,12},{9,13},{1... | collective-permute-start | bytes 393224 | tf_op jit(solution)/shard_map/ppermute | solution.py:45
  138.1 88.9 %copy-start.87 = (f32[128]{0:T(128)}, f32[128]{0:T(128)S(1)}, u32[]{:S(2)}) copy-start(f32[128]{0:T(128)S(1)} %add_divide_fusion.1) | copy-start | bytes 1540
  138.1 25.5 %collective-permute-start.22 = (f32[128,256]{1,0:T(8,128)S(1)}, f32[128,256]{1,0:T(8,128)}, u32[]{:S(2)}, u32[]{:S(2)}) collective-permute-start(f32[128,256]{1,0:T(8,128)S(1)} %bitcast.548), channel_id=1, source_target_pairs={{0,12},{1,13},{2,14},{3,15},{4,0},{5,1},{6,2},{7,3},{8,4},{9,5},{1... | collective-permute-start | bytes 393224 | tf_op jit(solution)/shard_map/ppermute | solution.py:45
  181.1 6.5 %collective-permute-start.23 = (f32[1,128,256]{2,1,0:T(8,128)S(1)}, f32[1,128,256]{2,1,0:T(8,128)S(1)}, u32[]{:S(2)}, u32[]{:S(2)}) collective-permute-start(f32[1,128,256]{2,1,0:T(8,128)S(1)} %get-tuple-element.21), channel_id=1, source_target_pairs={{0,16},{16,0},{1,17},{17,1},{2,18},{18,2},{3,19},{19,3},{4,20},{20... | collective-permute-start | bytes 393224 | tf_op jit(solution)/shard_map/ppermute | solution.py:34
  183.1 12.3 %collective-permute-start.24 = (f32[1,128,256]{2,1,0:T(8,128)}, f32[1,128,256]{2,1,0:T(8,128)}, u32[]{:S(2)}, u32[]{:S(2)}) collective-permute-start(f32[1,128,256]{2,1,0:T(8,128)} %get-tuple-element.17), channel_id=1, source_target_pairs={{16,0},{0,16},{17,1},{1,17},{18,2},{2,18},{19,3},{3,19},{20,4},{4,... | collective-permute-start | bytes 393224 | tf_op jit(solution)/shard_map/ppermute | solution.py:37
  183.2 16.3 %collective-permute-start.25 = (f32[1,128,256]{2,1,0:T(8,128)}, f32[1,128,256]{2,1,0:T(8,128)}, u32[]{:S(2)}, u32[]{:S(2)}) collective-permute-start(f32[1,128,256]{2,1,0:T(8,128)} %get-tuple-element.20), channel_id=1, source_target_pairs={{0,1},{1,2},{2,3},{3,4},{4,5},{5,6},{6,7},{7,8},{8,9},{9,10},{10,1... | collective-permute-start | bytes 393224 | tf_op jit(solution)/shard_map/ppermute | solution.py:34
  183.2 20.3 %collective-permute-start.26 = (f32[1,128,256]{2,1,0:T(8,128)}, f32[1,128,256]{2,1,0:T(8,128)}, u32[]{:S(2)}, u32[]{:S(2)}) collective-permute-start(f32[1,128,256]{2,1,0:T(8,128)} %get-tuple-element.18), channel_id=1, source_target_pairs={{1,0},{2,1},{3,2},{4,3},{5,4},{6,5},{7,6},{8,7},{9,8},{10,9},{11,1... | collective-permute-start | bytes 393224 | tf_op jit(solution)/shard_map/ppermute | solution.py:37
  187.6 19.9 %collective-permute-start.27 = (f32[128,256]{1,0:T(8,128)}, f32[128,256]{1,0:T(8,128)}, u32[]{:S(2)}, u32[]{:S(2)}) collective-permute-start(f32[128,256]{1,0:T(8,128)} %get-tuple-element.19), channel_id=1, source_target_pairs={{0,4},{1,5},{2,6},{3,7},{4,8},{5,9},{6,10},{7,11},{8,12},{9,13},{1... | collective-permute-start | bytes 393224 | tf_op jit(solution)/shard_map/ppermute | solution.py:45
  187.6 26.0 %collective-permute-start.28 = (f32[128,256]{1,0:T(8,128)}, f32[128,256]{1,0:T(8,128)}, u32[]{:S(2)}, u32[]{:S(2)}) collective-permute-start(f32[128,256]{1,0:T(8,128)} %get-tuple-element.16), channel_id=1, source_target_pairs={{0,12},{1,13},{2,14},{3,15},{4,0},{5,1},{6,2},{7,3},{8,4},{9,5},{1... | collective-permute-start | bytes 393224 | tf_op jit(solution)/shard_map/ppermute | solution.py:45
  228.7 85.9 %copy-start.86 = (f32[3,96]{1,0:T(4,128)S(1)}, f32[3,96]{1,0:T(4,128)}, u32[]{:S(2)}) copy-start(f32[3,96]{1,0:T(4,128)} %param.14) | copy-start | bytes 3460
  314.7 1.2 collective-permute-start.29
  315.9 3.9 %collective-permute-start.30 = (f32[128,6]{0,1:T(8,128)S(1)}, f32[128,6]{0,1:T(8,128)S(1)}, u32[]{:S(2)}, u32[]{:S(2)}) collective-permute-start(f32[128,6]{0,1:T(8,128)S(1)} %maximum_select_fusion.11), channel_id=1, source_target_pairs={{0,2},{1,3},{2,0},{3,1},{4,6},{5,7},{6,4},{7,5},{8,10},{9,11},{10,... | collective-permute-start | bytes 9224 | tf_op jit(solution)/shard_map/ppermute | solution.py:15
  319.8 3.7 collective-permute-start.31
  323.5 4.7 %collective-permute-start.32 = (f32[128,24]{0,1:T(8,128)S(1)}, f32[128,24]{0,1:T(8,128)S(1)}, u32[]{:S(2)}, u32[]{:S(2)}) collective-permute-start(f32[128,24]{0,1:T(8,128)S(1)} %maximum_select_fusion.7), channel_id=1, source_target_pairs={{0,8},{1,9},{2,10},{3,11},{4,12},{5,13},{6,14},{7,15},{8,0},{9,1},... | collective-permute-start | bytes 36872 | tf_op jit(solution)/shard_map/ppermute | solution.py:15
  328.2 3.8 collective-permute-start.33
  335.4 13.1 %collective-permute-start.34 = (f32[1,128,256]{2,1,0:T(8,128)S(1)}, f32[1,128,256]{2,1,0:T(8,128)S(1)}, u32[]{:S(2)}, u32[]{:S(2)}) collective-permute-start(f32[1,128,256]{2,1,0:T(8,128)S(1)} %bitcast.556), channel_id=1, source_target_pairs={{0,16},{16,0},{1,17},{17,1},{2,18},{18,2},{3,19},{19,3},{4,20},{20... | collective-permute-start | bytes 393224 | tf_op jit(solution)/shard_map/ppermute | solution.py:34
  338.4 18.2 %collective-permute-start.35 = (f32[1,128,256]{2,1,0:T(8,128)S(1)}, f32[1,128,256]{2,1,0:T(8,128)}, u32[]{:S(2)}, u32[]{:S(2)}) collective-permute-start(f32[1,128,256]{2,1,0:T(8,128)S(1)} %bitcast.557), channel_id=1, source_target_pairs={{16,0},{0,16},{17,1},{1,17},{18,2},{2,18},{19,3},{3,19},{20,4},{4,... | collective-permute-start | bytes 393224 | tf_op jit(solution)/shard_map/ppermute | solution.py:37
  339.5 19.8 %collective-permute-start.36 = (f32[1,128,256]{2,1,0:T(8,128)S(1)}, f32[1,128,256]{2,1,0:T(8,128)}, u32[]{:S(2)}, u32[]{:S(2)}) collective-permute-start(f32[1,128,256]{2,1,0:T(8,128)S(1)} %bitcast.554), channel_id=1, source_target_pairs={{0,1},{1,2},{2,3},{3,4},{4,5},{5,6},{6,7},{7,8},{8,9},{9,10},{10,1... | collective-permute-start | bytes 393224 | tf_op jit(solution)/shard_map/ppermute | solution.py:34
  340.6 21.4 %collective-permute-start.37 = (f32[1,128,256]{2,1,0:T(8,128)S(1)}, f32[1,128,256]{2,1,0:T(8,128)}, u32[]{:S(2)}, u32[]{:S(2)}) collective-permute-start(f32[1,128,256]{2,1,0:T(8,128)S(1)} %bitcast.555), channel_id=1, source_target_pairs={{1,0},{2,1},{3,2},{4,3},{5,4},{6,5},{7,6},{8,7},{9,8},{10,9},{11,1... | collective-permute-start | bytes 393224 | tf_op jit(solution)/shard_map/ppermute | solution.py:37
  346.1 18.5 %collective-permute-start.38 = (f32[128,256]{1,0:T(8,128)S(1)}, f32[128,256]{1,0:T(8,128)}, u32[]{:S(2)}, u32[]{:S(2)}) collective-permute-start(f32[128,256]{1,0:T(8,128)S(1)} %bitcast.553), channel_id=1, source_target_pairs={{0,4},{1,5},{2,6},{3,7},{4,8},{5,9},{6,10},{7,11},{8,12},{9,13},{1... | collective-permute-start | bytes 393224 | tf_op jit(solution)/shard_map/ppermute | solution.py:45
  348.4 18.9 %collective-permute-start.39 = (f32[128,256]{1,0:T(8,128)}, f32[128,256]{1,0:T(8,128)}, u32[]{:S(2)}, u32[]{:S(2)}) collective-permute-start(f32[128,256]{1,0:T(8,128)} %bitcast.149), channel_id=1, source_target_pairs={{0,12},{1,13},{2,14},{3,15},{4,0},{5,1},{6,2},{7,3},{8,4},{9,5},{1... | collective-permute-start | bytes 393224 | tf_op jit(solution)/shard_map/ppermute | solution.py:45
  (88 other events, 1806.9 us)
